TPU v7x, 512 devices: a whole 4x4x16 slice. The times are simulated.
512 devices in a mesh: line: 8 (over y_hi, x), bus: 32 (over y_lo, z), scen: 2 (over core).
Axes of the slice: x: 4, y: 4 (y_hi: 2, y_lo: 2; y = y_hi * 2 + y_lo), z: 16, core: 2. Of those that a mesh axis runs over, the one named last changes fastest.
Arguments:
- ptdf: bfloat16 [8192, 49152], P('line', 'bus'), may hold values from -0.0546875 to 0.0546875
- injections: bfloat16 [49152, 512], P('bus', 'scen'), may hold values from -6 to 6
- lodf: bfloat16 [8192, 2048], P(('line', 'bus')), may hold values from -3 to 3
- ratings: float32 [8192], P(('line', 'bus')), may hold values from 0.5 to 2
- outages: int32 [2048], replicated, may hold values from 0 to 8191, as said below
Outputs:
- overload: float32 [8192, 2048], P(('line', 'bus'))
Inputs may be any that keep to these rules, and one draw needn't show every extreme that they name: `outages`: 2048 distinct line indices.
All inputs are finite; a program needn't handle non-finite values.
Results may differ from a plain program's by a relative error of at most 0.0003.
Values sent between devices are 32-bit elements; how exact they have to be, the bound alone decides.
No kernel may reach another device: no remote copies, remote signals or barrier semaphores. Data moves between devices by JAX's collectives and lax.ppermute only.
A program may use at most 64 MiB of HBM per device.

v0:
```python
import jax
import jax.numpy as jnp
from jax import lax
from jax.sharding import PartitionSpec as P

softness = 0.2


def base_flow_term(base_rows, lodf_rows, outage_flow):
    return (
        base_rows[:, None, :] + lodf_rows.astype(jnp.float32)[:, :, None] * outage_flow[None, :, :]
    )


def overload_sum(base_flow, outage_flow, lodf, ratings):
    lines_here = base_flow.shape[0]
    groups = lines_here // 4

    def line_block(pieces):
        base_rows, lodf_rows, rating_rows = pieces
        post_flow = base_flow_term(base_rows, lodf_rows, outage_flow)
        margin = (jnp.abs(post_flow) - rating_rows[:, None, None]) / (
            softness * rating_rows[:, None, None]
        )
        return jnp.sum(jax.nn.sigmoid(margin), axis=2)

    summed = lax.map(
        line_block,
        (base_flow.reshape(groups, 4, -1), lodf.reshape(groups, 4, -1), ratings.reshape(groups, 4)),
    )
    return summed.reshape(lines_here, -1)


def select_rows(flows, outages, first):
    count = flows.shape[0]
    offset = outages - first
    inside = (offset >= 0) & (offset < count)
    picked = jnp.take(flows, jnp.clip(offset, 0, count - 1), axis=0)
    return jnp.where(inside[:, None], picked, 0.0)


def shards(ptdf, injections, lodf, ratings, outages):
    own_rows = lodf.shape[0]
    base_flow = lax.psum_scatter(
        jnp.dot(ptdf, injections, preferred_element_type=jnp.float32),
        "bus",
        scatter_dimension=0,
        tiled=True,
    )
    first_own = (lax.axis_index("line") * lax.axis_size("bus") + lax.axis_index("bus")) * own_rows
    outage_flow = lax.psum(select_rows(base_flow, outages, first_own), ("line", "bus"))
    local_sum = overload_sum(base_flow, outage_flow, lodf, ratings)
    total = lax.psum(local_sum, "scen")
    return total / (injections.shape[1] * lax.axis_size("scen"))


def solution(mesh):
    return jax.shard_map(
        shards,
        mesh=mesh,
        in_specs=(
            P("line", "bus"),
            P("bus", "scen"),
            P(("line", "bus"), None),
            P(("line", "bus")),
            P(),
        ),
        out_specs=P(("line", "bus"), None),
        check_vma=False,
    )
```

profile of v0, /device:TPU:1, one launch (start us, length us, event | category | flops | bytes accessed | tf_op | source)
XLA Modules:
  0.0 666.5 jit_solution(12721925452298086936)
XLA Ops:
  6.5 1.9 copy-done
  8.4 3.1 fusion.4
  11.5 0.0 reduce-scatter.2.cloned.1.call-update
  11.5 0.0 all-reduce.3.cloned.1.call-start
  11.6 118.5 %reduce-scatter.2.cloned.1.call-done = f32[32,256]{1,0:T(8,128)} async-done(((f32[1024,256]{1,0:T(8,128)}), f32[32,256]{1,0:T(8,128)}) %reduce-scatter.2.cloned.1.call-update) | async-done | bytes 32784 | tf_op jit(solution)/shard_map/reduce_scatter | solution.py:44
  130.1 9.3 %gather_fusion = f32[2048,256]{1,0:T(8,128)} fusion(f32[32,256]{1,0:T(8,128)} %reduce-scatter.2.cloned.1.call-done, s32[2048]{0:T(1024)S(1)} %fusion.2), kind=kCustom, calls=%fused_computation | custom fusion | bytes 4202496 | tf_op jit(solution)/shard_map/jit(_take)/gather | solution.py:38
  139.4 4.3 select_select_fusion
  143.8 0.0 all-reduce.3.cloned.1.call-update
  143.8 0.0 all-reduce.5.cloned.1.call-start
  143.9 0.1 reshape.38
  143.9 0.1 reshape.39
  144.0 420.5 %all-reduce.3.cloned.1.call-done = f32[2048,256]{1,0:T(8,128)} async-done(((f32[2048,256]{1,0:T(8,128)}), f32[2048,256]{1,0:T(8,128)}) %all-reduce.3.cloned.1.call-update) | async-done | bytes 2097168 | tf_op jit(solution)/shard_map/psum | solution.py:51
  564.5 46.5 %while.10 = (s32[]{:T(128)}, f32[8,4,2048]{2,1,0:T(4,128)}, f32[8,4,256]{2,1,0:T(4,128)S(1)}, bf16[8,4,2048]{2,1,0:T(4,128)(2,1)S(1)}, f32[2048,256]{1,0:T(8,128)}, /*index=5*/f32[8,4]{1,0:T(8,128)S(1)}, s32[]{:T(128)}) while((s32[]{:T(128)}, f32[8,4,2048]{2,1,0:T(4,128)}, f32[8,4,256]{2,1,0:T(4,128)S(1)}, bf16[8,4,2048]{2,1,0:T(4,128)(2,1)S(1)}, ...), condition=%wide.region_4.5_spmd, body=%wide.region_2.4_spmd.sunk | while | flops 18874372 | bytes 2290345 | solution.py:27
  564.5 5.1 fusion.8
  569.7 0.6 bitcast_dynamic-update-slice_fusion.2
  570.4 5.1 fusion.8
  575.5 0.6 bitcast_dynamic-update-slice_fusion.2
  576.2 5.1 fusion.8
  581.3 0.6 bitcast_dynamic-update-slice_fusion.2
  582.0 5.1 fusion.8
  587.1 0.6 bitcast_dynamic-update-slice_fusion.2
  587.8 5.1 fusion.8
  592.9 0.6 bitcast_dynamic-update-slice_fusion.2
  593.6 5.1 fusion.8
  598.7 0.6 bitcast_dynamic-update-slice_fusion.2
  599.4 5.1 fusion.8
  604.5 0.6 bitcast_dynamic-update-slice_fusion.2
  605.2 5.1 fusion.8
  610.4 0.6 bitcast_dynamic-update-slice_fusion.2
  611.0 1.7 reshape.40
  612.7 45.5 %all-reduce.5.cloned.1.call-done = f32[32,2048]{1,0:T(8,128)} async-done(((f32[32,2048]{1,0:T(8,128)}), f32[32,2048]{1,0:T(8,128)}) %all-reduce.5.cloned.1.call-update) | async-done | bytes 262160 | tf_op jit(solution)/shard_map/psum | solution.py:53
  658.3 1.7 broadcast_multiply_fusion.1
  (39 shorter events, 0.3 us)
Async XLA Ops:
  6.5 1.9 copy-start
  6.5 5.1 copy-start.3
  6.5 123.6 %reduce-scatter.2.cloned.1.call-start = ((), (), s32[]{:S(2)}) async-start(), calls=%async_computation.1 | async-start | bytes 1081344 | tf_op jit(solution)/shard_map/reduce_scatter | solution.py:44
  11.5 553.0 %all-reduce.3.cloned.1.call-start = ((), (), s32[]{:S(2)}) async-start(), calls=%async_computation.2 | async-start | bytes 4194304 | tf_op jit(solution)/shard_map/psum | solution.py:51
  139.4 4.4 copy-start.2
  139.4 4.5 copy-start.4
  139.4 4.6 copy-start.1
  143.8 514.5 %all-reduce.5.cloned.1.call-start = ((), (), s32[]{:S(2)}) async-start(), calls=%async_computation.3 | async-start | bytes 524288 | tf_op jit(solution)/shard_map/psum | solution.py:53
Sparse Core Ops, SparseCore 0:
  11.7 118.4 reduce-scatter.1
  143.9 420.5 all-reduce.2
  612.9 45.3 all-reduce.4
where the time goes:
time: 667 us; the launch traced here: 666 us
  waiting for transfers between devices  585 us (88%)
  other arithmetic  47.3 us (7%)
  local copies, waits for them, and re-layouts  18.2 us (3%)
  between operations  13.2 us (2%)
    psum x1, waiting for transfers between devices, shards(): lax.psum(select_rows(base_flow, outages, first_own), ('line', 'bus'))  420 us
    reduce_scatter x1, waiting for transfers between devices, shards(): lax.psum_scatter(jnp.dot(ptdf, injections, preferred_element_type=jnp.flo...  118 us
    psum x1, waiting for transfers between devices, shards(): total = lax.psum(local_sum, 'scen')  45.5 us
    reduce_sum x8, other arithmetic, line_block(): return jnp.sum(jax.nn.sigmoid(margin), axis=2)  41.2 us
  transfers between devices with their start and end apart: 3, of which 3 were waited for; matrix products, arithmetic and copies ran while one was open for 0% of the time, Pallas kernels for 0%

commit v1 on v0

--- a/solution.py
+++ b/solution.py
@@ -48,7 +48,7 @@
         tiled=True,
     )
     first_own = (lax.axis_index("line") * lax.axis_size("bus") + lax.axis_index("bus")) * own_rows
-    outage_flow = lax.psum(select_rows(base_flow, outages, first_own), ("line", "bus"))
+    outage_flow = lax.psum(lax.psum(select_rows(base_flow, outages, first_own), "line"), "bus")
     local_sum = overload_sum(base_flow, outage_flow, lodf, ratings)
     total = lax.psum(local_sum, "scen")
     return total / (injections.shape[1] * lax.axis_size("scen"))

time: 667 us -> 625 us (0.937)
  waiting for transfers between devices: 585 us -> 542 us
    psum x1 -> x2, waiting for transfers between devices: 420 us -> 367 us  [the longest x1 248 us: shards(): lax.psum(lax.psum(select_rows(base_flow, outages, first_own), 'line'), 'b...]
    psum x1, waiting for transfers between devices: 45.5 us -> 55.9 us  [shards(): total = lax.psum(local_sum, 'scen')]
  transfers between devices with their start and end apart: 3 -> 4, of which waited for: 3 -> 4; matrix products, arithmetic and copies ran while one was open for 0% -> 0% of each run, Pallas kernels for 0% -> 0%
where the time goes in v1:
time: 625 us; the launch traced here: 624 us
  waiting for transfers between devices  542 us (87%)
  other arithmetic  47.3 us (8%)
  local copies, waits for them, and re-layouts  18.2 us (3%)
  between operations  13.2 us (2%)
    psum x1, waiting for transfers between devices, shards(): lax.psum(lax.psum(select_rows(base_flow, outages, first_own), 'line'), 'b...  248 us
    psum x1, waiting for transfers between devices, shards(): lax.psum(select_rows(base_flow, outages, first_own), 'line')  119 us
    reduce_scatter x1, waiting for transfers between devices, shards(): lax.psum_scatter(jnp.dot(ptdf, injections, preferred_element_type=jnp.flo...  118 us
    psum x1, waiting for transfers between devices, shards(): total = lax.psum(local_sum, 'scen')  55.9 us
    reduce_sum x8, other arithmetic, line_block(): return jnp.sum(jax.nn.sigmoid(margin), axis=2)  41.3 us
  transfers between devices with their start and end apart: 4, of which 4 were waited for; matrix products, arithmetic and copies ran while one was open for 0% of the time, Pallas kernels for 0%

profile of v1, /device:TPU:1, one launch (start us, length us, event | category | flops | bytes accessed | tf_op | source)
XLA Modules:
  0.0 623.8 jit_solution(5935915449818516128)
XLA Ops:
  6.5 1.9 copy-done
  8.4 3.1 fusion.4
  11.5 0.0 all-reduce.4.cloned.1.call-start
  11.6 118.5 %reduce-scatter.2.cloned.1.call-done = f32[32,256]{1,0:T(8,128)} async-done(((f32[1024,256]{1,0:T(8,128)}), f32[32,256]{1,0:T(8,128)}) %reduce-scatter.2.cloned.1.call-update) | async-done | bytes 32784 | tf_op jit(solution)/shard_map/reduce_scatter | solution.py:44
  130.1 9.3 %gather_fusion = f32[2048,256]{1,0:T(8,128)} fusion(f32[32,256]{1,0:T(8,128)} %reduce-scatter.2.cloned.1.call-done, s32[2048]{0:T(1024)S(1)} %fusion.2), kind=kCustom, calls=%fused_computation | custom fusion | bytes 4202496 | tf_op jit(solution)/shard_map/jit(_take)/gather | solution.py:38
  139.4 4.3 select_select_fusion
  143.8 0.0 all-reduce.6.cloned.1.call-start
  143.8 119.2 %all-reduce.4.cloned.1.call-done = f32[2048,256]{1,0:T(8,128)} async-done(((f32[2048,256]{1,0:T(8,128)}), f32[2048,256]{1,0:T(8,128)}) %all-reduce.4.cloned.1.call-update) | async-done | bytes 2097168 | tf_op jit(solution)/shard_map/psum | solution.py:51
  263.1 0.0 all-reduce.8.cloned.1.call-start
  263.1 0.1 reshape.38
  263.2 0.1 reshape.39
  263.3 248.0 %all-reduce.6.cloned.1.call-done = f32[2048,256]{1,0:T(8,128)} async-done(((f32[2048,256]{1,0:T(8,128)}), f32[2048,256]{1,0:T(8,128)}) %all-reduce.6.cloned.1.call-update) | async-done | bytes 2097168 | tf_op jit(solution)/shard_map/psum | solution.py:51
  511.3 46.6 %while.10 = (s32[]{:T(128)}, f32[8,4,2048]{2,1,0:T(4,128)}, f32[8,4,256]{2,1,0:T(4,128)S(1)}, bf16[8,4,2048]{2,1,0:T(4,128)(2,1)S(1)}, f32[2048,256]{1,0:T(8,128)}, /*index=5*/f32[8,4]{1,0:T(8,128)S(1)}, s32[]{:T(128)}) while((s32[]{:T(128)}, f32[8,4,2048]{2,1,0:T(4,128)}, f32[8,4,256]{2,1,0:T(4,128)S(1)}, bf16[8,4,2048]{2,1,0:T(4,128)(2,1)S(1)}, ...), condition=%wide.region_5.6_spmd, body=%wide.region_3.5_spmd.sunk | while | flops 18874372 | bytes 2290345 | solution.py:27
  511.3 5.2 fusion.8
  516.5 0.6 bitcast_dynamic-update-slice_fusion.2
  517.1 5.2 fusion.8
  522.3 0.6 bitcast_dynamic-update-slice_fusion.2
  523.0 5.2 fusion.8
  528.1 0.6 bitcast_dynamic-update-slice_fusion.2
  528.8 5.2 fusion.8
  533.9 0.6 bitcast_dynamic-update-slice_fusion.2
  534.6 5.2 fusion.8
  539.8 0.6 bitcast_dynamic-update-slice_fusion.2
  540.4 5.2 fusion.8
  545.6 0.6 bitcast_dynamic-update-slice_fusion.2
  546.2 5.2 fusion.8
  551.4 0.6 bitcast_dynamic-update-slice_fusion.2
  552.1 5.2 fusion.8
  557.2 0.6 bitcast_dynamic-update-slice_fusion.2
  557.8 1.7 reshape.40
  559.6 55.9 %all-reduce.8.cloned.1.call-done = f32[32,2048]{1,0:T(8,128)} async-done(((f32[32,2048]{1,0:T(8,128)}), f32[32,2048]{1,0:T(8,128)}) %all-reduce.8.cloned.1.call-update) | async-done | bytes 262160 | tf_op jit(solution)/shard_map/psum | solution.py:53
  615.5 1.7 broadcast_multiply_fusion.1
  (42 shorter events, 0.3 us)
Async XLA Ops:
  6.5 1.9 copy-start
  6.5 5.1 copy-start.3
  6.5 123.6 %reduce-scatter.2.cloned.1.call-start = ((), (), s32[]{:S(2)}) async-start(), calls=%async_computation.1 | async-start | bytes 1081344 | tf_op jit(solution)/shard_map/reduce_scatter | solution.py:44
  11.5 251.5 %all-reduce.4.cloned.1.call-start = ((), (), s32[]{:S(2)}) async-start(), calls=%async_computation.2 | async-start | bytes 4194304 | tf_op jit(solution)/shard_map/psum | solution.py:51
  143.7 119.4 %copy-start.2 = (bf16[32,2048]{1,0:T(8,128)(2,1)S(1)}, bf16[32,2048]{1,0:T(8,128)(2,1)}, u32[]{:S(2)}) copy-start(bf16[32,2048]{1,0:T(8,128)(2,1)} %param.9) | copy-start | bytes 393220
  143.7 119.5 %copy-start.4 = (f32[32]{0:T(128)S(1)}, f32[32]{0:T(128)}, u32[]{:S(2)}) copy-start(f32[32]{0:T(128)} %param.10) | copy-start | bytes 388
  143.7 119.5 %copy-start.1 = (f32[32,256]{1,0:T(8,128)S(1)}, f32[32,256]{1,0:T(8,128)}, u32[]{:S(2)}) copy-start(f32[32,256]{1,0:T(8,128)} %reduce-scatter.2.cloned.1.call-done) | copy-start | bytes 98308
  143.8 367.5 %all-reduce.6.cloned.1.call-start = ((), (), s32[]{:S(2)}) async-start(), calls=%async_computation.3 | async-start | bytes 4194304 | tf_op jit(solution)/shard_map/psum | solution.py:51
  263.1 352.5 %all-reduce.8.cloned.1.call-start = ((), (), s32[]{:S(2)}) async-start(), calls=%async_computation.4 | async-start | bytes 524288 | tf_op jit(solution)/shard_map/psum | solution.py:53
Sparse Core Ops, SparseCore 0:
  11.7 118.4 reduce-scatter.1
  143.9 119.1 all-reduce.3
  266.0 245.2 all-reduce.5
  559.7 55.7 all-reduce.7
